TPU v7x, 32 devices: a whole 2x2x4 slice. The times are simulated.
32 devices in a mesh: arc: 8 (over z, x), vec: 4 (over y, core).
Axes of the slice: x: 2, y: 2, z: 4, core: 2. Of those that a mesh axis runs over, the one named last changes fastest.
Arguments:
- right_side: float32 [640, 128, 128], P(('arc', 'vec')), may hold values from -6 to 6
- prior_diag: float32 [640, 128], P(('arc', 'vec')), may hold values from 0.5 to 4
- inv_factor: bfloat16 [512, 256, 256], P(('arc', 'vec'))
- coupling_panel: bfloat16 [512, 256, 1024], P(('arc', 'vec')), may hold values from -0.09375 to 0.09375
- coupling_owner: int32 [512, 8], replicated, may hold values from 0 to 31, all different within a row; in each aligned block of 16 rows (0 to 15, 16 to 31, ...) at most 5 rows name the same one
- coupling_block: int32 [512, 8], replicated, may hold values from 0 to 19
Outputs:
- solution_field: float32 [640, 128, 128], P(('arc', 'vec'))
- residual: float32 [640, 128, 128], P(('arc', 'vec'))
Inputs may be any that keep to these rules, and one draw needn't show every extreme that they name: `coupling_owner`: the 8 holders named for one arc are different. Among the 16 arcs of one device (aligned blocks of rows) no holder is named more than 5 times; some holder is named exactly 5 times.
All inputs are finite; a program needn't handle non-finite values.
Results may differ from a plain program's by a relative error of at most 0.006.
The roundings to bfloat16 on the way count: a program that leaves them out, or rounds other values in their place, can miss the bound.
Values may be sent and summed in bfloat16 or wider, within the bound.
No kernel may reach another device: no remote copies, remote signals or barrier semaphores. Data moves between devices by JAX's collectives and lax.ppermute only.
A program may use at most 128 MiB of HBM per device.

v0:
```python
import jax
import jax.numpy as jnp
from jax import lax
from jax.sharding import PartitionSpec as P

ITERS = 2


def inner_gram(left, right):
    return jnp.einsum("grc,grd->cd", left, right, precision=lax.Precision.HIGHEST)


def combine_cols(field, weights):
    return jnp.einsum("grc,cd->grd", field, weights, precision=lax.Precision.HIGHEST)


def times_high(left, right):
    return jnp.dot(left, right, precision=lax.Precision.HIGHEST)


def trade_out(buffer):
    return lax.all_to_all(buffer, ("arc", "vec"), split_axis=0, concat_axis=0, tiled=True)


def trade_back(buffer):
    return lax.all_to_all(buffer, ("arc", "vec"), split_axis=0, concat_axis=0, tiled=True)


def per_device(right_side, prior_diag, inv_factor, coupling_panel, coupling_owner, coupling_block):
    device_count = lax.axis_size(("arc", "vec"))
    my_index = lax.axis_index(("arc", "vec"))
    arcs_here = coupling_panel.shape[0]
    links = coupling_owner.shape[1]
    blocks_here = right_side.shape[0]
    block_rows = right_side.shape[1]
    rhs_count = right_side.shape[2]
    entries = arcs_here * links
    slot_count = (entries + device_count - 1) // device_count + 1
    owner_all = coupling_owner.reshape(device_count, entries)
    block_all = coupling_block.reshape(device_count, entries)
    position = jnp.arange(entries, dtype=jnp.int32)
    earlier = (owner_all[:, :, None] == owner_all[:, None, :]) & (
        position[None, None, :] < position[None, :, None]
    )
    rank_all = jnp.sum(earlier.astype(jnp.int32), axis=2)
    owner_mine = lax.dynamic_index_in_dim(owner_all, my_index, 0, keepdims=False)
    rank_mine = lax.dynamic_index_in_dim(rank_all, my_index, 0, keepdims=False)
    slot_mine = owner_mine * slot_count + rank_mine
    slot_ids = jnp.arange(slot_count, dtype=jnp.int32)
    matches = (owner_all[:, None, :] == my_index) & (
        rank_all[:, None, :] == slot_ids[None, :, None]
    )
    filled = jnp.any(matches, axis=2).reshape(-1)
    source_block = jnp.sum(jnp.where(matches, block_all[:, None, :], 0), axis=2).reshape(-1)
    block_ids = jnp.arange(blocks_here, dtype=jnp.int32)
    selector = ((source_block[:, None] == block_ids[None, :]) & filled[:, None]).astype(
        jnp.bfloat16
    )
    solution_field = jnp.zeros_like(right_side)
    residual = right_side
    direction = right_side
    res_gram = lax.psum(inner_gram(residual, residual), ("arc", "vec"))
    for sweep_index in range(ITERS):
        local_rounded = direction.astype(jnp.bfloat16)
        outgoing = jnp.where(
            filled[:, None, None], local_rounded[source_block], jnp.zeros((), jnp.bfloat16)
        )
        arrived = trade_out(outgoing)
        fetched = arrived[slot_mine].reshape(arcs_here, links * block_rows, rhs_count)
        coupled = jnp.einsum(
            "apk,akc->apc", coupling_panel, fetched, preferred_element_type=jnp.float32
        ).astype(jnp.bfloat16)
        whitened = jnp.einsum(
            "apq,aqc->apc", inv_factor, coupled, preferred_element_type=jnp.float32
        ).astype(jnp.bfloat16)
        smoothed = jnp.einsum(
            "aqp,aqc->apc", inv_factor, whitened, preferred_element_type=jnp.float32
        ).astype(jnp.bfloat16)
        projected = jnp.einsum(
            "apk,apc->akc", coupling_panel, smoothed, preferred_element_type=jnp.float32
        ).astype(jnp.bfloat16)
        projected = projected.reshape(entries, block_rows, rhs_count)
        returning = (
            jnp.zeros((device_count * slot_count, block_rows, rhs_count), jnp.bfloat16)
            .at[slot_mine]
            .set(projected)
        )
        came_back = trade_back(returning)
        summed = jnp.einsum("sb,src->brc", selector, came_back, preferred_element_type=jnp.float32)
        image_vec = prior_diag[:, :, None] * direction + summed
        curv_gram, image_gram, cross_gram = lax.psum(
            (
                inner_gram(direction, image_vec),
                inner_gram(image_vec, image_vec),
                inner_gram(residual, image_vec),
            ),
            ("arc", "vec"),
        )
        factor_low = jnp.linalg.cholesky(curv_gram)
        step_mat = jax.scipy.linalg.cho_solve((factor_low, True), res_gram)
        solution_field = solution_field + combine_cols(direction, step_mat)
        residual = residual - combine_cols(image_vec, step_mat)
        if sweep_index + 1 < ITERS:
            new_gram = (
                res_gram - times_high(step_mat.T, cross_gram.T) - times_high(cross_gram, step_mat)
            )
            new_gram = new_gram + times_high(step_mat.T, times_high(image_gram, step_mat))
            beta_mat = jax.scipy.linalg.cho_solve((jnp.linalg.cholesky(res_gram), True), new_gram)
            direction = residual + combine_cols(direction, beta_mat)
            res_gram = new_gram
    return (solution_field, residual)


def solution(mesh):
    in_specs = (
        P(("arc", "vec"), None, None),
        P(("arc", "vec"), None),
        P(("arc", "vec"), None, None),
        P(("arc", "vec"), None, None),
        P(),
        P(),
    )
    out_specs = (P(("arc", "vec"), None, None), P(("arc", "vec"), None, None))
    return jax.shard_map(
        per_device, mesh=mesh, in_specs=in_specs, out_specs=out_specs, check_vma=False
    )
```

profile of v0, /device:TPU:0, one launch (start us, length us, event | category | flops | bytes accessed | tf_op | source)
XLA Modules:
  0.0 1013.6 jit_solution(7668285359423061608)
XLA Ops:
  7.2 1.7 copy.142
  10.1 1.3 convert_reduce_fusion
  11.8 1.6 copy.143
  15.8 8.8 gather_fusion
  24.6 5.3 broadcast_select_fusion.1
  29.9 7.5 all-to-all-start
  37.4 117.0 %all-to-all-done = bf16[160,128,128]{2,1,0:T(8,128)(2,1)} async-done(((bf16[160,128,128]{2,1,0:T(8,128)(2,1)}), bf16[160,128,128]{2,1,0:T(8,128)(2,1)}, u32[]{:S(2)}, u32[]{:S(2)}) %all-to-all-start) | async-done | bytes 5242912 | tf_op jit(solution)/shard_map/all_to_all | solution.py:22
  154.3 5.6 gather_fusion.1
  159.9 9.2 convolution_convert_fusion.4
  169.1 7.3 convert_bitcast_fusion.1
  176.4 6.4 copy.148
  182.8 3.7 broadcast.116.clone
  186.5 19.4 %scatter_fusion = bf16[160,128,128]{2,1,0:T(8,128)(2,1)} fusion(bf16[160,128,128]{2,1,0:T(8,128)(2,1)} %broadcast.116.clone, s32[128]{0:T(128)S(1)} %fusion.35, bf16[128,128,128]{2,1,0:T(8,128)(2,1)} %bitcast.113), kind=kCustom, calls=%fused_computation.4 | custom fusion | bytes 12583424 | tf_op jit(solution)/shard_map/scatter | solution.py:86
  205.9 5.5 all-to-all-start.1
  211.7 2.9 convolution_bitcast_fusion.6
  214.6 113.8 %all-to-all-done.1 = bf16[160,128,128]{2,1,0:T(8,128)(2,1)} async-done(((bf16[160,128,128]{2,1,0:T(8,128)(2,1)}), bf16[160,128,128]{2,1,0:T(8,128)(2,1)}, u32[]{:S(2)}, u32[]{:S(2)}) %all-to-all-start.1) | async-done | bytes 5242912 | tf_op jit(solution)/shard_map/all_to_all | solution.py:26
  328.4 5.4 fusion.2
  333.7 3.6 convolution_bitcast_fusion.5
  337.3 3.5 convolution_bitcast_fusion.7
  341.3 126.2 %all-reduce.6.cloned.1.call-done = (f32[128,128]{0,1:T(8,128)}, f32[128,128]{0,1:T(8,128)}, f32[128,128]{1,0:T(8,128)}) async-done(((f32[128,128]{0,1:T(8,128)}, f32[128,128]{0,1:T(8,128)}, f32[128,128]{1,0:T(8,128)}), (f32[128,128]{0,1:T(8,128)}, f32[128,128]{0,1:T(8,128)}, f32[128,128]{1,0:T(8,128)})) %all-reduce.6.cloned.1.call-update) | async-done | bytes 196624 | tf_op jit(solution)/shard_map/psum | solution.py:62
  469.4 1.5 fusion.19
  470.9 12.5 %cholesky.59 = f32[128,128]{1,0:T(8,128)S(1)} custom-call(f32[128,128]{1,0:T(8,128)} %get-tuple-element.20), custom_call_target="Cholesky" | custom-call | tf_op jit(solution)/shard_map/jit(cholesky)/cholesky | solution.py:99
  485.5 10.6 %custom-call.9 = f32[1,128,128]{1,2,0:T(8,128)S(1)} custom-call(f32[1,128,128]{2,1,0:T(8,128)} %fusion.9), custom_call_target="InvertDiagBlocksLowerTriangular" | custom-call | tf_op jit(solution)/shard_map/jit(_cho_solve)/triangular_solve | solution.py:100
  497.5 1.8 convolution_subtract_fusion.3
  499.2 3.8 convolution_subtract_fusion.1
  503.1 13.2 %cholesky.70 = f32[128,128]{1,0:T(8,128)} custom-call(f32[128,128]{1,0:T(8,128)} %get-tuple-element.19), custom_call_target="Cholesky" | custom-call | tf_op jit(solution)/shard_map/jit(cholesky)/cholesky | solution.py:108
  517.8 2.1 fusion.10
  519.9 11.4 %custom-call.10 = f32[1,128,128]{1,2,0:T(8,128)} custom-call(f32[1,128,128]{2,1,0:T(8,128)} %fusion.10), custom_call_target="InvertDiagBlocksLowerTriangular" | custom-call | tf_op jit(solution)/shard_map/jit(_cho_solve)/triangular_solve | solution.py:108
  536.0 3.8 fusion.36
  539.8 8.9 gather_fusion.2
  548.7 2.9 broadcast_select_fusion
  551.6 121.7 %all_to_all.20 = bf16[160,128,128]{2,1,0:T(8,128)(2,1)} all-to-all(bf16[160,128,128]{2,1,0:T(8,128)(2,1)S(1)} %broadcast_select_fusion), channel_id=1, replica_groups=mesh['arc'=8,'vec'=4] {'arc','vec'}, dimensions={0} | all-to-all | bytes 10485760 | tf_op jit(solution)/shard_map/all_to_all | solution.py:22
  673.3 5.7 gather_fusion.3
  679.0 9.2 convolution_convert_fusion.1
  688.2 7.2 convert_bitcast_fusion
  695.4 6.5 copy.164
  701.9 3.6 broadcast.116
  705.5 19.5 %scatter_fusion.1 = bf16[160,128,128]{2,1,0:T(8,128)(2,1)} fusion(bf16[160,128,128]{2,1,0:T(8,128)(2,1)} %broadcast.116, s32[128]{0:T(128)} %copy-done.12, bf16[128,128,128]{2,1,0:T(8,128)(2,1)} %bitcast.112), kind=kCustom, calls=%fused_computation.5 | custom fusion | bytes 12583424 | tf_op jit(solution)/shard_map/scatter | solution.py:86
  725.0 119.8 %all_to_all.21 = bf16[160,128,128]{2,1,0:T(8,128)(2,1)S(1)} all-to-all(bf16[160,128,128]{2,1,0:T(8,128)(2,1)} %scatter_fusion.1), channel_id=1, replica_groups=mesh['arc'=8,'vec'=4] {'arc','vec'}, dimensions={0} | all-to-all | bytes 10485760 | tf_op jit(solution)/shard_map/all_to_all | solution.py:26
  844.8 2.9 fusion
  848.8 3.5 convolution_bitcast_fusion.4
  852.4 2.4 convolution_bitcast_fusion.1
  854.8 116.3 %all-reduce.4.cloned.1.call-done = f32[128,128]{0,1:T(8,128)} async-done(((f32[128,128]{0,1:T(8,128)}), f32[128,128]{0,1:T(8,128)}) %all-reduce.4.cloned.1.call-update) | async-done | bytes 65552 | tf_op jit(solution)/shard_map/psum | solution.py:91
  972.9 11.7 %cholesky.81 = f32[128,128]{1,0:T(8,128)S(1)} custom-call(f32[128,128]{1,0:T(8,128)S(1)} %fusion.15), custom_call_target="Cholesky" | custom-call | tf_op jit(solution)/shard_map/jit(cholesky)/cholesky | solution.py:99
  985.9 10.0 custom-call.11
  996.5 4.7 convolution_subtract_fusion
  1001.2 2.4 convolution_add_fusion
  1003.6 2.8 copy.171
  (69 shorter events, 21.1 us)
Async XLA Ops:
  7.2 152.8 %copy-start = (bf16[16,256,256]{2,1,0:T(8,128)(2,1)S(1)}, bf16[16,256,256]{2,1,0:T(8,128)(2,1)}, u32[]{:S(2)}) copy-start(bf16[16,256,256]{2,1,0:T(8,128)(2,1)} %param.11) | copy-start | bytes 6291460
  7.2 7.6 copy-start.1
  14.8 9.8 copy-start.11
  29.9 124.5 %all-to-all-start = ((bf16[160,128,128]{2,1,0:T(8,128)(2,1)}), bf16[160,128,128]{2,1,0:T(8,128)(2,1)}, u32[]{:S(2)}, u32[]{:S(2)}) async-start(bf16[160,128,128]{2,1,0:T(8,128)(2,1)} %broadcast_select_fusion.1), calls=%async_computation | async-start | bytes 10485760 | tf_op jit(solution)/shard_map/all_to_all | solution.py:22
  37.3 149.1 %copy-start.12 = (s32[128]{0:T(128)}, s32[128]{0:T(128)S(1)}, u32[]{:S(2)}) copy-start(s32[128]{0:T(128)S(1)} %fusion.35) | copy-start | bytes 1540
  37.4 122.5 %copy-start.13 = (s32[1024]{0:T(1024)}, s32[1024]{0:T(1024)S(1)}, u32[]{:S(2)}) copy-start(s32[1024]{0:T(1024)S(1)} %pad_clamp_fusion) | copy-start | bytes 12292
  205.9 122.5 %all-to-all-start.1 = ((bf16[160,128,128]{2,1,0:T(8,128)(2,1)}), bf16[160,128,128]{2,1,0:T(8,128)(2,1)}, u32[]{:S(2)}, u32[]{:S(2)}) async-start(bf16[160,128,128]{2,1,0:T(8,128)(2,1)} %scatter_fusion), calls=%async_computation.1 | async-start | bytes 10485760 | tf_op jit(solution)/shard_map/all_to_all | solution.py:26
  211.3 256.2 %all-reduce.6.cloned.1.call-start = ((), (), s32[]{:S(2)}) async-start(), calls=%async_computation.5 | async-start | bytes 393216 | tf_op jit(solution)/shard_map/psum | solution.py:62
  211.7 122.0 %copy-start.9 = (s32[160]{0:T(256)}, s32[160]{0:T(256)S(1)}, u32[]{:S(2)}) copy-start(s32[160]{0:T(256)S(1)} %eq.60) | copy-start | bytes 1924
  214.6 119.2 %copy-start.8 = (f32[20,128]{1,0:T(8,128)S(1)}, f32[20,128]{1,0:T(8,128)}, u32[]{:S(2)}) copy-start(f32[20,128]{1,0:T(8,128)} %param.10) | copy-start | bytes 30724
  333.7 3.6 copy-start.4
  340.8 630.2 %all-reduce.4.cloned.1.call-start = ((), (), s32[]{:S(2)}) async-start(), calls=%async_computation.4 | async-start | bytes 131072 | tf_op jit(solution)/shard_map/psum | solution.py:91
  499.2 33.1 %copy-start.7 = (f32[128,128]{0,1:T(8,128)S(1)}, f32[128,128]{0,1:T(8,128)}, u32[]{:S(2)}) copy-start(f32[128,128]{0,1:T(8,128)} %get-tuple-element.15) | copy-start | bytes 196612
  725.0 119.8 %copy-start.10 = (s32[160]{0:T(256)S(1)}, s32[160]{0:T(256)}, u32[]{:S(2)}) copy-start(s32[160]{0:T(256)} %copy-done.9) | copy-start | bytes 1924
  844.8 4.1 copy-start.2
  847.7 1.2 copy-start.5
  996.4 4.7 copy-start.3
  996.5 4.7 copy-start.6
Sparse Core Ops, SparseCore 0:
  341.0 126.5 all-reduce.5
  852.5 118.5 all-reduce.3
where the time goes:
time: 1030 us; the launch traced here: 1010 us
  waiting for transfers between devices  473 us (46%)
  blocking collectives  241 us (23%)
  local copies, waits for them, and re-layouts  101 us (10%)
  other arithmetic  89.7 us (9%)
  matrix products  80 us (8%)
  between operations  14.8 us (1%)
  starting transfers between devices  13.7 us (1%)
    psum x1, waiting for transfers between devices, per_device(): res_gram = lax.psum(inner_gram(residual, residual), ('arc', 'vec'))  126 us
    all_to_all x1, blocking collectives, trade_out(): lax.all_to_all(buffer, ('arc', 'vec'), split_axis=0, concat_axis=0, tiled...  122 us
    all_to_all x1, blocking collectives, trade_back(): lax.all_to_all(buffer, ('arc', 'vec'), split_axis=0, concat_axis=0, tiled...  120 us
    all_to_all x1, waiting for transfers between devices, trade_out(): lax.all_to_all(buffer, ('arc', 'vec'), split_axis=0, concat_axis=0, tiled...  117 us
    psum x1, waiting for transfers between devices, per_device(): lax.psum((inner_gram(direction, image_vec), inner_gram(image_vec, image_v...  116 us
    all_to_all x1, waiting for transfers between devices, trade_back(): lax.all_to_all(buffer, ('arc', 'vec'), split_axis=0, concat_axis=0, tiled...  114 us
    scatter x2, local copies, waits for them, and re-layouts, per_device(): returning = jnp.zeros((device_count * slot_count, block_rows, rhs_count),...  38.8 us
    another operation x6, other arithmetic, per_device(): factor_low = jnp.linalg.cholesky(curv_gram)  25.7 us
  transfers between devices with their start and end apart: 4, of which 4 were waited for; matrix products, arithmetic and copies ran while one was open for 1% of the time, Pallas kernels for 0%

commit v1 on v0

--- a/solution.py
+++ b/solution.py
@@ -24,6 +24,17 @@
 
 def trade_back(buffer):
     return lax.all_to_all(buffer, ("arc", "vec"), split_axis=0, concat_axis=0, tiled=True)
+
+
+def sum_all(grams):
+    device_count = lax.axis_size(("arc", "vec"))
+    stacked = jnp.concatenate(grams, axis=0)
+    rows, cols = stacked.shape
+    pieces = stacked.reshape(device_count, rows // device_count, cols)
+    mine = jnp.sum(trade_out(pieces), axis=0)
+    shared = jnp.broadcast_to(mine[None], pieces.shape)
+    total = trade_out(shared).reshape(len(grams), rows // len(grams), cols)
+    return [total[i] for i in range(len(grams))]
 
 
 def per_device(right_side, prior_diag, inv_factor, coupling_panel, coupling_owner, coupling_block):
@@ -59,7 +70,7 @@
     solution_field = jnp.zeros_like(right_side)
     residual = right_side
     direction = right_side
-    res_gram = lax.psum(inner_gram(residual, residual), ("arc", "vec"))
+    (res_gram,) = sum_all([inner_gram(residual, residual)])
     for sweep_index in range(ITERS):
         local_rounded = direction.astype(jnp.bfloat16)
         outgoing = jnp.where(
@@ -88,14 +99,17 @@
         came_back = trade_back(returning)
         summed = jnp.einsum("sb,src->brc", selector, came_back, preferred_element_type=jnp.float32)
         image_vec = prior_diag[:, :, None] * direction + summed
-        curv_gram, image_gram, cross_gram = lax.psum(
-            (
-                inner_gram(direction, image_vec),
-                inner_gram(image_vec, image_vec),
-                inner_gram(residual, image_vec),
-            ),
-            ("arc", "vec"),
-        )
+        last = sweep_index + 1 == ITERS
+        if last:
+            (curv_gram,) = sum_all([inner_gram(direction, image_vec)])
+        else:
+            curv_gram, image_gram, cross_gram = sum_all(
+                [
+                    inner_gram(direction, image_vec),
+                    inner_gram(image_vec, image_vec),
+                    inner_gram(residual, image_vec),
+                ]
+            )
         factor_low = jnp.linalg.cholesky(curv_gram)
         step_mat = jax.scipy.linalg.cho_solve((factor_low, True), res_gram)
         solution_field = solution_field + combine_cols(direction, step_mat)

time: 1030 us -> 809 us (0.79)
  waiting for transfers between devices: 473 us -> 235 us
  starting transfers between devices: 13.7 us -> 40.6 us
  between operations: 14.8 us -> 1.34 us
  blocking collectives: 241 us -> 253 us
    psum x2 -> x0, waiting for transfers between devices: 243 us -> none  [the longest x1 126 us: per_device(): res_gram = lax.psum(inner_gram(residual, residual), ('arc', 'vec'))]
    all_to_all x1 -> x6, starting transfers between devices: 7.45 us -> 34.5 us  [trade_out(): lax.all_to_all(buffer, ('arc', 'vec'), split_axis=0, concat_axis=0, tiled...]
    all_to_all x1 -> x2, blocking collectives: 122 us -> 133 us  [trade_out(): lax.all_to_all(buffer, ('arc', 'vec'), split_axis=0, concat_axis=0, tiled...]
    all_to_all x1 -> x6, waiting for transfers between devices: 117 us -> 119 us  [trade_out(): lax.all_to_all(buffer, ('arc', 'vec'), split_axis=0, concat_axis=0, tiled...]
  transfers between devices with their start and end apart: 4 -> 7, of which waited for: 4 -> 3; matrix products, arithmetic and copies ran while one was open for 1% -> 12% of each run, Pallas kernels for 0% -> 0%
where the time goes in v1:
time: 809 us; the launch traced here: 801 us
  blocking collectives  253 us (31%)
  waiting for transfers between devices  235 us (29%)
  local copies, waits for them, and re-layouts  107 us (13%)
  other arithmetic  90.7 us (11%)
  matrix products  73.3 us (9%)
  starting transfers between devices  40.6 us (5%)
    all_to_all x2, blocking collectives, trade_out(): lax.all_to_all(buffer, ('arc', 'vec'), split_axis=0, concat_axis=0, tiled...  133 us
    all_to_all x1, blocking collectives, trade_back(): lax.all_to_all(buffer, ('arc', 'vec'), split_axis=0, concat_axis=0, tiled...  120 us
    all_to_all x6, waiting for transfers between devices, trade_out(): lax.all_to_all(buffer, ('arc', 'vec'), split_axis=0, concat_axis=0, tiled...  119 us
    all_to_all x1, waiting for transfers between devices, trade_back(): lax.all_to_all(buffer, ('arc', 'vec'), split_axis=0, concat_axis=0, tiled...  116 us
    scatter x2, local copies, waits for them, and re-layouts, per_device(): returning = jnp.zeros((device_count * slot_count, block_rows, rhs_count),...  38.8 us
    all_to_all x6, starting transfers between devices, trade_out(): lax.all_to_all(buffer, ('arc', 'vec'), split_axis=0, concat_axis=0, tiled...  34.5 us
    another operation x6, other arithmetic, per_device(): factor_low = jnp.linalg.cholesky(curv_gram)  25.7 us
    another operation x4, other arithmetic, per_device(): step_mat = jax.scipy.linalg.cho_solve((factor_low, True), res_gram)  22.3 us
  transfers between devices with their start and end apart: 7, of which 3 were waited for; matrix products, arithmetic and copies ran while one was open for 12% of the time, Pallas kernels for 0%

profile of v1, /device:TPU:0, one launch (start us, length us, event | category | flops | bytes accessed | tf_op | source)
XLA Modules:
  0.0 801.4 jit_solution(7875241467822307250)
XLA Ops:
  0.7 1.7 copy.136
  9.3 8.8 %gather_fusion = bf16[160,128,128]{2,1,0:T(8,128)(2,1)} fusion(bf16[20,128,128]{2,1,0:T(8,128)(2,1)} %convert_element_type.47, s32[1024]{0:T(1024)S(1)} %pad_clamp_fusion.1), kind=kCustom, calls=%fused_computation | custom fusion | bytes 10486400 | tf_op jit(solution)/shard_map/gather | solution.py:77
  18.1 5.3 broadcast_select_fusion.1
  23.3 7.5 all-to-all-start
  30.8 2.9 fusion.39
  33.7 114.1 %all-to-all-done = bf16[160,128,128]{2,1,0:T(8,128)(2,1)} async-done(((bf16[160,128,128]{2,1,0:T(8,128)(2,1)}), bf16[160,128,128]{2,1,0:T(8,128)(2,1)}, u32[]{:S(2)}, u32[]{:S(2)}) %all-to-all-start) | async-done | bytes 5242912 | tf_op jit(solution)/shard_map/all_to_all | solution.py:22
  147.8 5.6 all-to-all-start.4
  153.4 5.6 gather_fusion.1
  159.0 9.2 %convolution_convert_fusion.4 = bf16[16,128,256]{2,1,0:T(8,128)(2,1)} fusion(bf16[16,256,256]{2,1,0:T(8,128)(2,1)S(1)} %copy-done, bf16[16,1024,128]{2,1,0:T(8,128)(2,1)} %bitcast.127, bf16[16,256,1024]{2,1,0:T(8,128)(2,1)} %param.12), kind=kOutput, calls=%fused_computation.19 | convolution fusion | flops 1343225856 | bytes 15728640 | tf_op jit(solution)/shard_map/apq,aqc->apc/dot_general | solution.py:84
  168.2 7.3 convert_bitcast_fusion.1
  175.4 6.4 copy.142
  181.8 3.7 broadcast.119.clone
  185.5 19.4 %scatter_fusion = bf16[160,128,128]{2,1,0:T(8,128)(2,1)} fusion(bf16[160,128,128]{2,1,0:T(8,128)(2,1)} %broadcast.119.clone, s32[128]{0:T(128)S(1)} %fusion.37, bf16[128,128,128]{2,1,0:T(8,128)(2,1)} %bitcast.125), kind=kCustom, calls=%fused_computation.4 | custom fusion | bytes 12583424 | tf_op jit(solution)/shard_map/scatter | solution.py:97
  204.9 6.0 all-to-all-start.1
  211.6 116.3 %all-to-all-done.1 = bf16[160,128,128]{2,1,0:T(8,128)(2,1)} async-done(((bf16[160,128,128]{2,1,0:T(8,128)(2,1)}), bf16[160,128,128]{2,1,0:T(8,128)(2,1)}, u32[]{:S(2)}, u32[]{:S(2)}) %all-to-all-start.1) | async-done | bytes 5242912 | tf_op jit(solution)/shard_map/all_to_all | solution.py:26
  328.6 5.6 all-to-all-start.5
  334.2 5.4 fusion.2
  339.6 2.6 convolution_bitcast_fusion.5
  342.2 3.0 convolution_bitcast_fusion.4
  347.6 6.1 all-to-all-start.2
  354.4 12.5 %cholesky.70 = f32[128,128]{1,0:T(8,128)S(1)} custom-call(f32[128,128]{1,0:T(8,128)} %fusion.22), custom_call_target="Cholesky" | custom-call | tf_op jit(solution)/shard_map/jit(cholesky)/cholesky | solution.py:122
  369.9 6.4 all-to-all-start.3
  378.2 11.3 %custom-call.10 = f32[1,128,128]{1,2,0:T(8,128)} custom-call(f32[1,128,128]{2,1,0:T(8,128)} %fusion.11), custom_call_target="InvertDiagBlocksLowerTriangular" | custom-call | tf_op jit(solution)/shard_map/jit(_cho_solve)/triangular_solve | solution.py:122
  395.0 12.5 %cholesky.59 = f32[128,128]{1,0:T(8,128)S(1)} custom-call(f32[128,128]{1,0:T(8,128)} %fusion.14), custom_call_target="Cholesky" | custom-call | tf_op jit(solution)/shard_map/jit(cholesky)/cholesky | solution.py:113
  409.5 10.6 %custom-call.9 = f32[1,128,128]{1,2,0:T(8,128)S(1)} custom-call(f32[1,128,128]{2,1,0:T(8,128)} %fusion.10), custom_call_target="InvertDiagBlocksLowerTriangular" | custom-call | tf_op jit(solution)/shard_map/jit(_cho_solve)/triangular_solve | solution.py:114
  424.3 2.8 convolution_subtract_fusion.1
  429.2 2.7 fusion.38
  431.9 8.9 %gather_fusion.2 = bf16[160,128,128]{2,1,0:T(8,128)(2,1)} fusion(bf16[20,128,128]{2,1,0:T(8,128)(2,1)} %get-tuple-element.14, s32[1024]{0:T(1024)} %copy-done.12), kind=kCustom, calls=%fused_computation.2 | custom fusion | bytes 10486400 | tf_op jit(solution)/shard_map/gather | solution.py:77
  440.8 2.9 broadcast_select_fusion
  443.7 121.8 %all_to_all.50 = bf16[160,128,128]{2,1,0:T(8,128)(2,1)} all-to-all(bf16[160,128,128]{2,1,0:T(8,128)(2,1)S(1)} %broadcast_select_fusion), channel_id=1, replica_groups=mesh['arc'=8,'vec'=4] {'arc','vec'}, dimensions={0} | all-to-all | bytes 10485760 | tf_op jit(solution)/shard_map/all_to_all | solution.py:22
  565.5 5.7 gather_fusion.3
  571.2 9.2 %convolution_convert_fusion.1 = bf16[16,128,256]{2,1,0:T(8,128)(2,1)} fusion(bf16[16,256,256]{2,1,0:T(8,128)(2,1)S(1)} %copy-done, bf16[16,1024,128]{2,1,0:T(8,128)(2,1)} %bitcast.126, bf16[16,256,1024]{2,1,0:T(8,128)(2,1)} %param.12), kind=kOutput, calls=%fused_computation.16 | convolution fusion | flops 1343225856 | bytes 15728640 | tf_op jit(solution)/shard_map/apq,aqc->apc/dot_general | solution.py:84
  580.4 7.2 convert_bitcast_fusion
  587.6 6.5 copy.155
  594.1 3.6 broadcast.119
  597.7 19.4 %scatter_fusion.1 = bf16[160,128,128]{2,1,0:T(8,128)(2,1)} fusion(bf16[160,128,128]{2,1,0:T(8,128)(2,1)} %broadcast.119, s32[128]{0:T(128)} %copy-done.13, bf16[128,128,128]{2,1,0:T(8,128)(2,1)} %bitcast.124), kind=kCustom, calls=%fused_computation.5 | custom fusion | bytes 12583424 | tf_op jit(solution)/shard_map/scatter | solution.py:97
  617.1 119.9 %all_to_all.51 = bf16[160,128,128]{2,1,0:T(8,128)(2,1)S(1)} all-to-all(bf16[160,128,128]{2,1,0:T(8,128)(2,1)} %scatter_fusion.1), channel_id=1, replica_groups=mesh['arc'=8,'vec'=4] {'arc','vec'}, dimensions={0} | all-to-all | bytes 10485760 | tf_op jit(solution)/shard_map/all_to_all | solution.py:26
  737.0 2.9 fusion
  739.9 2.8 fusion.5
  742.7 11.0 %all_to_all.52 = f32[32,4,128]{2,1,0:T(4,128)} all-to-all(f32[32,4,128]{2,1,0:T(4,128)S(1)} %bitcast.132), channel_id=1, replica_groups=mesh['arc'=8,'vec'=4] {'arc','vec'}, dimensions={0} | all-to-all | bytes 131072 | tf_op jit(solution)/shard_map/all_to_all | solution.py:22
  755.2 3.5 all-to-all-start.9
  758.7 2.4 convolution_bitcast_fusion.1
  761.1 5.0 all-to-all-done.9
  767.9 11.7 %cholesky.81 = f32[128,128]{1,0:T(8,128)S(1)} custom-call(f32[128,128]{1,0:T(8,128)S(1)} %fusion.18), custom_call_target="Cholesky" | custom-call | tf_op jit(solution)/shard_map/jit(cholesky)/cholesky | solution.py:113
  780.9 9.8 %custom-call.11 = f32[1,128,128]{1,2,0:T(8,128)S(1)} custom-call(f32[1,128,128]{2,1,0:T(8,128)S(1)} %fusion.12), custom_call_target="InvertDiagBlocksLowerTriangular" | custom-call | tf_op jit(solution)/shard_map/jit(_cho_solve)/triangular_solve | solution.py:114
  791.3 4.7 convolution_subtract_fusion
  796.0 2.4 convolution_add_fusion
  798.4 2.8 copy.161
  (87 shorter events, 34.9 us)
Async XLA Ops:
  0.6 158.3 %copy-start = (bf16[16,256,256]{2,1,0:T(8,128)(2,1)S(1)}, bf16[16,256,256]{2,1,0:T(8,128)(2,1)}, u32[]{:S(2)}) copy-start(bf16[16,256,256]{2,1,0:T(8,128)(2,1)} %param.11) | copy-start | bytes 6291460
  0.6 7.6 copy-start.1
  8.3 9.8 %copy-start.12 = (s32[1024]{0:T(1024)}, s32[1024]{0:T(1024)S(1)}, u32[]{:S(2)}) copy-start(s32[1024]{0:T(1024)S(1)} %pad_clamp_fusion.1) | copy-start | bytes 12292
  23.3 124.5 %all-to-all-start = ((bf16[160,128,128]{2,1,0:T(8,128)(2,1)}), bf16[160,128,128]{2,1,0:T(8,128)(2,1)}, u32[]{:S(2)}, u32[]{:S(2)}) async-start(bf16[160,128,128]{2,1,0:T(8,128)(2,1)} %broadcast_select_fusion.1), calls=%async_computation | async-start | bytes 10485760 | tf_op jit(solution)/shard_map/all_to_all | solution.py:22
  30.8 154.7 %copy-start.13 = (s32[128]{0:T(128)}, s32[128]{0:T(128)S(1)}, u32[]{:S(2)}) copy-start(s32[128]{0:T(128)S(1)} %fusion.37) | copy-start | bytes 1540
  30.8 128.1 %copy-start.14 = (s32[1024]{0:T(1024)}, s32[1024]{0:T(1024)S(1)}, u32[]{:S(2)}) copy-start(s32[1024]{0:T(1024)S(1)} %pad_clamp_fusion) | copy-start | bytes 12292
  147.8 57.1 %all-to-all-start.4 = ((f32[32,4,128]{2,1,0:T(4,128)}), f32[32,4,128]{2,1,0:T(4,128)S(1)}, u32[]{:S(2)}, u32[]{:S(2)}) async-start(f32[32,4,128]{2,1,0:T(4,128)} %bitcast.15), calls=%async_computation.4 | async-start | bytes 131072 | tf_op jit(solution)/shard_map/all_to_all | solution.py:22
  204.9 123.1 %all-to-all-start.1 = ((bf16[160,128,128]{2,1,0:T(8,128)(2,1)}), bf16[160,128,128]{2,1,0:T(8,128)(2,1)}, u32[]{:S(2)}, u32[]{:S(2)}) async-start(bf16[160,128,128]{2,1,0:T(8,128)(2,1)} %scatter_fusion), calls=%async_computation.1 | async-start | bytes 10485760 | tf_op jit(solution)/shard_map/all_to_all | solution.py:26
  328.6 19.0 %all-to-all-start.5 = ((f32[32,4,128]{2,1,0:T(4,128)}), f32[32,4,128]{2,1,0:T(4,128)S(1)}, u32[]{:S(2)}, u32[]{:S(2)}) async-start(f32[32,4,128]{2,1,0:T(4,128)} %broadcast_in_dim.40), calls=%async_computation.5 | async-start | bytes 131072 | tf_op jit(solution)/shard_map/all_to_all | solution.py:22
  334.2 5.4 copy-start.8
  339.6 5.6 copy-start.4
  347.6 19.4 %all-to-all-start.2 = ((f32[32,12,128]{2,1,0:T(8,128)}), f32[32,12,128]{2,1,0:T(8,128)}, u32[]{:S(2)}, u32[]{:S(2)}) async-start(f32[32,12,128]{2,1,0:T(8,128)} %reshape.138), calls=%async_computation.2 | async-start | bytes 524288 | tf_op jit(solution)/shard_map/all_to_all | solution.py:22
  369.9 19.5 %all-to-all-start.3 = ((f32[32,12,128]{2,1,0:T(8,128)}), f32[32,12,128]{2,1,0:T(8,128)}, u32[]{:S(2)}, u32[]{:S(2)}) async-start(f32[32,12,128]{2,1,0:T(8,128)} %broadcast_in_dim.39), calls=%async_computation.3 | async-start | bytes 524288 | tf_op jit(solution)/shard_map/all_to_all | solution.py:22
  420.2 0.6 copy-start.10
  424.3 4.3 copy-start.9
  427.2 4.7 copy-start.5
  617.1 119.9 %copy-start.11 = (s32[160]{0:T(256)S(1)}, s32[160]{0:T(256)}, u32[]{:S(2)}) copy-start(s32[160]{0:T(256)} %eq.60) | copy-start | bytes 1924
  737.0 2.9 copy-start.2
  739.9 2.8 copy-start.6
  755.2 10.9 %all-to-all-start.9 = ((f32[32,4,128]{2,1,0:T(4,128)}), f32[32,4,128]{2,1,0:T(4,128)}, u32[]{:S(2)}, u32[]{:S(2)}) async-start(f32[32,4,128]{2,1,0:T(4,128)} %broadcast_in_dim.41), calls=%async_computation.9 | async-start | bytes 131072 | tf_op jit(solution)/shard_map/all_to_all | solution.py:22
  791.2 4.7 copy-start.3
  791.3 4.7 copy-start.7

commit v2 on v1

v2 whole, which is shorter than its diff:
```python
import functools

import jax
import jax.numpy as jnp
from jax import lax
from jax.experimental import pallas as pl
from jax.experimental.pallas import tpu as pltpu
from jax.sharding import PartitionSpec as P

ITERS = 2
AXES = ("arc", "vec")
SMEM = pltpu.MemorySpace.SMEM
VMEM = pltpu.MemorySpace.VMEM


def inner_gram(left, right):
    return jnp.einsum("grc,grd->cd", left, right, precision=lax.Precision.HIGHEST)


def combine_cols(field, weights):
    return jnp.einsum("grc,cd->grd", field, weights, precision=lax.Precision.HIGHEST)


def times_high(left, right):
    return jnp.dot(left, right, precision=lax.Precision.HIGHEST)


def trade(buffer):
    return lax.all_to_all(buffer, AXES, split_axis=0, concat_axis=0, tiled=True)


def sum_all(grams):
    device_count = lax.axis_size(AXES)
    stacked = jnp.concatenate(grams, axis=0)
    rows, cols = stacked.shape
    pieces = stacked.reshape(device_count, rows // device_count, cols)
    mine = jnp.sum(trade(pieces), axis=0)
    shared = jnp.broadcast_to(mine[None], pieces.shape)
    total = trade(shared).reshape(len(grams), rows // len(grams), cols)
    return [total[i] for i in range(len(grams))]


class Plan:
    def __init__(self, mesh, arcs_here, links, blocks_here):
        arc, vec = mesh.shape["arc"], mesh.shape["vec"]
        half = max(1, vec // 2)
        self.rings = arc // half if arc % half == 0 else arc
        self.devices = arc * vec
        self.plane = self.devices // self.rings
        self.arcs, self.links, self.blocks = arcs_here, links, blocks_here
        entries = arcs_here * links
        self.cap = (entries + self.devices - 1) // self.devices + 1
        self.slots = self.plane * self.cap
        self.pos_row = self.slots
        self.own_row = self.slots + arcs_here
        self.rows = self.slots + 2 * arcs_here
        self.order = [self.plane_at(i) for i in range(self.rings)]
        self.ring = [
            (self.order[i] * self.plane + p, self.order[(i + 1) % self.rings] * self.plane + p)
            for i in range(self.rings)
            for p in range(self.plane)
        ]
        self.groups = [
            [z * self.plane + p for p in range(self.plane)] for z in range(self.rings)
        ]

    def plane_at(self, place):
        return 2 * place if 2 * place < self.rings else 2 * self.rings - 1 - 2 * place

    def place_of(self, z):
        half = lax.div(z, 2)
        return jnp.where(lax.rem(z, 2) == 0, half, self.rings - 1 - half)

    def source_plane(self, me, step):
        place = self.place_of(lax.div(me, self.plane))
        place = lax.rem(place - step + self.rings, self.rings)
        doubled = 2 * place
        return jnp.where(doubled < self.rings, doubled, 2 * self.rings - 1 - doubled)


def tables_kernel(plan, me_ref, owner_ref, block_ref, tab_ref):
    me = me_ref[0]
    arcs, links, lanes = plan.arcs, plan.links, tab_ref.shape[1]
    z = lax.div(me, plan.plane)
    owners = lax.broadcasted_iota(jnp.int32, (arcs, lanes), 1)
    low = lax.broadcasted_iota(jnp.int32, (arcs, arcs), 0)
    high = lax.broadcasted_iota(jnp.int32, (arcs, arcs), 1)
    before = (high < low).astype(jnp.float32)

    def incidence(row):
        owner = owner_ref[pl.ds(row, arcs), :]
        block = block_ref[pl.ds(row, arcs), :]
        named = jnp.zeros((arcs, lanes), jnp.float32)
        held = jnp.zeros((arcs, lanes), jnp.int32)
        for k in range(links):
            same = owner[:, k : k + 1] == owners
            named = jnp.where(same, 1.0, named)
            held = jnp.where(same, block[:, k : k + 1] + 1, held)
        rank = jnp.dot(before, named, preferred_element_type=jnp.float32).astype(jnp.int32)
        return held, rank

    for q in range(plan.plane):
        row = pl.multiple_of((z * plan.plane + q) * arcs, arcs)
        held, rank = incidence(row)
        for r in range(plan.cap):
            at_rank = jnp.where(rank == r, held, 0)
            tab_ref[r * plan.plane + q : r * plan.plane + q + 1, :] = jnp.sum(
                at_rank, axis=0, keepdims=True
            )
    row = pl.multiple_of(me * arcs, arcs)
    held, rank = incidence(row)
    place = plan.place_of(z)
    other = plan.place_of(lax.div(owners, plan.plane))
    step = lax.rem(place - other + plan.rings, plan.rings)
    slot = step * plan.slots + lax.rem(owners, plan.plane) * plan.cap + rank
    tab_ref[plan.pos_row : plan.pos_row + arcs, :] = slot
    mine = jnp.zeros((arcs, lanes), jnp.int32)
    owner = owner_ref[pl.ds(row, arcs), :]
    for k in range(links):
        mine = jnp.where(owners == k, owner[:, k : k + 1], mine)
    tab_ref[plan.own_row : plan.own_row + arcs, :] = mine


def make_tables(plan, me, coupling_owner, coupling_block):
    lanes = -(-plan.devices // 128) * 128
    return pl.pallas_call(
        functools.partial(tables_kernel, plan),
        out_shape=jax.ShapeDtypeStruct((plan.rows, lanes), jnp.int32),
        in_specs=[
            pl.BlockSpec(memory_space=SMEM),
            pl.BlockSpec(memory_space=VMEM),
            pl.BlockSpec(memory_space=VMEM),
        ],
        out_specs=pl.BlockSpec(memory_space=VMEM),
        name="tables",
    )(me, coupling_owner, coupling_block)


def pick_kernel(plan, step, me_ref, tab_ref, chunk_ref, out_ref):
    me = me_ref[0]
    column = plan.source_plane(me, step) * plan.plane + lax.rem(me, plan.plane)

    @pl.loop(0, plan.plane)
    def _(q):
        for r in range(plan.cap):
            block = jnp.maximum(tab_ref[r * plan.plane + q, column] - 1, 0)
            out_ref[q * plan.cap + r] = chunk_ref[block]


def pick(plan, step, me, tab, chunk):
    shape = (plan.slots,) + chunk.shape[1:]
    return pl.pallas_call(
        functools.partial(pick_kernel, plan, step),
        out_shape=jax.ShapeDtypeStruct(shape, chunk.dtype),
        in_specs=[
            pl.BlockSpec(memory_space=SMEM),
            pl.BlockSpec(memory_space=SMEM),
            pl.BlockSpec(memory_space=VMEM),
        ],
        out_specs=pl.BlockSpec(memory_space=VMEM),
        name="pick",
    )(me, tab, chunk)


def arcs_kernel(plan, tab_ref, *refs):
    rings, slots = plan.rings, plan.slots
    arrived_refs = refs[:rings]
    panel_ref, factor_ref = refs[rings], refs[rings + 1]
    out_refs = refs[rings + 2 : 2 * rings + 2]
    arrived, leaving, fetched, sems = refs[2 * rings + 2 :]
    arc = pl.program_id(0)
    rows = arrived.shape[1]

    def inward(s):
        return pltpu.make_async_copy(
            arrived_refs[s], arrived.at[pl.ds(s * slots, slots)], sems.at[s]
        )

    def outward(s):
        return pltpu.make_async_copy(
            leaving.at[pl.ds(s * slots, slots)], out_refs[s], sems.at[s]
        )

    @pl.when(arc == 0)
    def _():
        for s in range(rings):
            inward(s).start()
        for s in range(rings):
            inward(s).wait()

    spots = []
    for k in range(plan.links):
        spot = tab_ref[plan.pos_row + arc, tab_ref[plan.own_row + arc, k]]
        spots.append(spot)
        fetched[k * rows : (k + 1) * rows, :] = arrived[spot]
    panel, factor = panel_ref[0], factor_ref[0]
    coupled = jnp.dot(panel, fetched[...], preferred_element_type=jnp.float32)
    coupled = coupled.astype(jnp.bfloat16)
    whitened = jnp.dot(factor, coupled, preferred_element_type=jnp.float32)
    whitened = whitened.astype(jnp.bfloat16)
    smoothed = lax.dot_general(
        whitened, factor, (((0,), (0,)), ((), ())), preferred_element_type=jnp.float32
    ).astype(jnp.bfloat16)
    projected = jnp.dot(smoothed, panel, preferred_element_type=jnp.float32)
    projected = projected.astype(jnp.bfloat16)
    for k in range(plan.links):
        leaving[spots[k]] = projected[:, k * rows : (k + 1) * rows]

    @pl.when(arc == pl.num_programs(0) - 1)
    def _():
        for s in range(rings):
            outward(s).start()
        for s in range(rings):
            outward(s).wait()


def run_arcs(plan, tab, arrived, coupling_panel, inv_factor):
    arcs, arc_rows, width = coupling_panel.shape
    block = arrived[0].shape[1:]
    total = plan.rings * plan.slots
    anywhere = pl.BlockSpec(memory_space=pl.ANY)
    return pl.pallas_call(
        functools.partial(arcs_kernel, plan),
        grid_spec=pltpu.PrefetchScalarGridSpec(
            num_scalar_prefetch=1,
            grid=(arcs,),
            in_specs=[anywhere] * plan.rings
            + [
                pl.BlockSpec((1, arc_rows, width), lambda i, t: (i, 0, 0)),
                pl.BlockSpec((1, arc_rows, arc_rows), lambda i, t: (i, 0, 0)),
            ],
            out_specs=[anywhere] * plan.rings,
            scratch_shapes=[
                pltpu.VMEM((total,) + block, jnp.bfloat16),
                pltpu.VMEM((total,) + block, jnp.bfloat16),
                pltpu.VMEM((width, block[1]), jnp.bfloat16),
                pltpu.SemaphoreType.DMA((plan.rings,)),
            ],
        ),
        out_shape=[jax.ShapeDtypeStruct((plan.slots,) + block, jnp.bfloat16)] * plan.rings,
        name="arcs",
    )(tab, *arrived, coupling_panel, inv_factor)


def fold_kernel(plan, step, has_prev, last, me_ref, tab_ref, got_ref, *refs):
    me = me_ref[0]
    prev_ref = refs[0] if has_prev else None
    out_ref, acc = refs[-2], refs[-1]
    column = plan.source_plane(me, step) * plan.plane + lax.rem(me, plan.plane)
    if has_prev:
        acc[...] = prev_ref[...].astype(jnp.float32)
    else:
        acc[...] = jnp.zeros_like(acc)

    @pl.loop(0, plan.plane)
    def _(q):
        for r in range(plan.cap):
            held = tab_ref[r * plan.plane + q, column]

            @pl.when(held > 0)
            def _():
                acc[held - 1] += got_ref[q * plan.cap + r].astype(jnp.float32)

    if last:

        @pl.loop(0, plan.blocks)
        def _(b):
            out_ref[b] = acc[b].T
    else:
        out_ref[...] = acc[...].astype(out_ref.dtype)


def fold(plan, step, me, tab, got, prev, last):
    shape = (plan.blocks,) + got.shape[1:]
    args = (me, tab, got) + (() if prev is None else (prev,))
    specs = [pl.BlockSpec(memory_space=SMEM)] * 2 + [pl.BlockSpec(memory_space=VMEM)] * (
        len(args) - 2
    )
    return pl.pallas_call(
        functools.partial(fold_kernel, plan, step, prev is not None, last),
        out_shape=jax.ShapeDtypeStruct(shape, jnp.float32 if last else jnp.bfloat16),
        in_specs=specs,
        out_specs=pl.BlockSpec(memory_space=VMEM),
        scratch_shapes=[pltpu.VMEM(shape, jnp.float32)],
        name="fold",
    )(*args)


def trade_plane(plan, buffer):
    return lax.all_to_all(
        buffer, AXES, split_axis=0, concat_axis=0, tiled=True, axis_index_groups=plan.groups
    )


def coupled_sum(plan, me, tab, rounded, coupling_panel, inv_factor):
    chunk, arrived = rounded, []
    for s in range(plan.rings):
        following = None
        if s + 1 < plan.rings:
            following = lax.ppermute(chunk, AXES, plan.ring)
        chosen = pick(plan, s, me, tab, chunk)
        arrived.append(trade_plane(plan, chosen))
        chunk = following
    leaving = run_arcs(plan, tab, arrived, coupling_panel, inv_factor)
    carried = None
    for j in range(plan.rings):
        s = (j + 1) % plan.rings
        last = j + 1 == plan.rings
        got = trade_plane(plan, leaving[s])
        carried = fold(plan, s, me, tab, got, carried, last)
        if not last:
            carried = lax.ppermute(carried, AXES, plan.ring)
    return carried


def per_device(
    mesh, right_side, prior_diag, inv_factor, coupling_panel, coupling_owner, coupling_block
):
    plan = Plan(mesh, coupling_panel.shape[0], coupling_owner.shape[1], right_side.shape[0])
    me = lax.axis_index(AXES).astype(jnp.int32).reshape(1)
    tab = make_tables(plan, me, coupling_owner, coupling_block)
    solution_field = jnp.zeros_like(right_side)
    residual = right_side
    direction = right_side
    (res_gram,) = sum_all([inner_gram(residual, residual)])
    for sweep_index in range(ITERS):
        summed = coupled_sum(
            plan, me, tab, direction.astype(jnp.bfloat16), coupling_panel, inv_factor
        )
        image_vec = prior_diag[:, :, None] * direction + summed
        last = sweep_index + 1 == ITERS
        if last:
            (curv_gram,) = sum_all([inner_gram(direction, image_vec)])
        else:
            curv_gram, image_gram, cross_gram = sum_all(
                [
                    inner_gram(direction, image_vec),
                    inner_gram(image_vec, image_vec),
                    inner_gram(residual, image_vec),
                ]
            )
        factor_low = jnp.linalg.cholesky(curv_gram)
        step_mat = jax.scipy.linalg.cho_solve((factor_low, True), res_gram)
        solution_field = solution_field + combine_cols(direction, step_mat)
        residual = residual - combine_cols(image_vec, step_mat)
        if not last:
            new_gram = (
                res_gram - times_high(step_mat.T, cross_gram.T) - times_high(cross_gram, step_mat)
            )
            new_gram = new_gram + times_high(step_mat.T, times_high(image_gram, step_mat))
            beta_mat = jax.scipy.linalg.cho_solve((jnp.linalg.cholesky(res_gram), True), new_gram)
            direction = residual + combine_cols(direction, beta_mat)
            res_gram = new_gram
    return (solution_field, residual)


def solution(mesh):
    in_specs = (
        P(AXES, None, None),
        P(AXES, None),
        P(AXES, None, None),
        P(AXES, None, None),
        P(),
        P(),
    )
    out_specs = (P(AXES, None, None), P(AXES, None, None))
    return jax.shard_map(
        functools.partial(per_device, mesh),
        mesh=mesh,
        in_specs=in_specs,
        out_specs=out_specs,
        check_vma=False,
    )
```

time: 809 us -> 631 us (0.78)
  blocking collectives: 253 us -> 119 us
  Pallas kernels: 0 us -> 96.9 us
  local copies, waits for them, and re-layouts: 107 us -> 19.6 us
  starting transfers between devices: 40.6 us -> 107 us
  waiting for transfers between devices: 235 us -> 179 us
  matrix products: 73.3 us -> 28.7 us
  other arithmetic: 90.7 us -> 71 us
    all_to_all x7 -> x16, waiting for transfers between devices: 235 us -> 21.2 us  [the longest x11 16.2 us: trade_plane(): lax.all_to_all(buffer, AXES, split_axis=0, concat_axis=0, tiled=True, axi...]
    ppermute x0 -> x12, waiting for transfers between devices: none -> 157 us  [the longest x6 87.9 us: coupled_sum(): following = lax.ppermute(chunk, AXES, plan.ring)]
    all_to_all x3 -> x6, blocking collectives: 253 us -> 119 us  [the longest x5 107 us: trade_plane(): lax.all_to_all(buffer, AXES, split_axis=0, concat_axis=0, tiled=True, axi...]
    pallas_call x0 -> x19, Pallas kernels: none -> 96.9 us  [the longest x2 45.8 us: run_arcs(): pl.pallas_call(functools.partial(arcs_kernel, plan), grid_spec=pltpu.Pref...]
    dot_general x6 -> x0, matrix products: 41.2 us -> none  [the longest x2 18.4 us: per_device(): jnp.einsum('apq,aqc->apc', inv_factor, coupled, preferred_element_type=jn...]
    scatter x2 -> x0, local copies, waits for them, and re-layouts: 38.8 us -> none  [per_device(): returning = jnp.zeros((device_count * slot_count, block_rows, rhs_count),...]
    ppermute x0 -> x12, starting transfers between devices: none -> 38.6 us  [the longest x6 19.4 us: coupled_sum(): carried = lax.ppermute(carried, AXES, plan.ring)]
    gather x4 -> x0, local copies, waits for them, and re-layouts: 29 us -> none  [the longest x2 17.7 us: per_device(): local_rounded[source_block]]
  transfers between devices with their start and end apart: 7 -> 28, of which waited for: 3 -> 16; matrix products, arithmetic and copies ran while one was open for 12% -> 6% of each run, Pallas kernels for 0% -> 10%
where the time goes in v2:
time: 631 us; the launch traced here: 623 us
  waiting for transfers between devices  179 us (28%)
  blocking collectives  119 us (19%)
  starting transfers between devices  107 us (17%)
  Pallas kernels  96.9 us (15%)
  other arithmetic  71 us (11%)
  matrix products  28.7 us (5%)
  local copies, waits for them, and re-layouts  19.6 us (3%)
    all_to_all x5, blocking collectives, trade_plane(): lax.all_to_all(buffer, AXES, split_axis=0, concat_axis=0, tiled=True, axi...  107 us
    ppermute x6, waiting for transfers between devices, coupled_sum(): following = lax.ppermute(chunk, AXES, plan.ring)  87.9 us
    ppermute x6, waiting for transfers between devices, coupled_sum(): carried = lax.ppermute(carried, AXES, plan.ring)  69.4 us
    all_to_all x11, starting transfers between devices, trade_plane(): lax.all_to_all(buffer, AXES, split_axis=0, concat_axis=0, tiled=True, axi...  46.9 us
    pallas_call x2, Pallas kernels, run_arcs(): pl.pallas_call(functools.partial(arcs_kernel, plan), grid_spec=pltpu.Pref...  45.8 us
    pallas_call x8, Pallas kernels, fold(): pl.pallas_call(functools.partial(fold_kernel, plan, step, prev is not Non...  28.8 us
    another operation x6, other arithmetic, per_device(): factor_low = jnp.linalg.cholesky(curv_gram)  24.8 us
    all_to_all x5, starting transfers between devices, trade(): return lax.all_to_all(buffer, AXES, split_axis=0, concat_axis=0, tiled=True)  21.7 us
  transfers between devices with their start and end apart: 28, of which 16 were waited for; matrix products, arithmetic and copies ran while one was open for 6% of the time, Pallas kernels for 10%

profile of v2, /device:TPU:0, one launch (start us, length us, event | category | flops | bytes accessed | tf_op | source)
XLA Modules:
  0.0 622.7 jit_solution(16728099386280531276)
XLA Ops:
  10.7 5.3 all-to-all-start
  18.7 14.6 %collective-permute-done.chunk_ref = bf16[20,128,128]{2,1,0:T(8,128)(2,1)S(1)} collective-permute-done((bf16[20,128,128]{2,1,0:T(8,128)(2,1)S(1)}, bf16[20,128,128]{2,1,0:T(8,128)(2,1)S(1)}, u32[]{:S(2)}, u32[]{:S(2)}) %collective-permute-start) | collective-permute-done | bytes 655392 | tf_op jit(solution)/shard_map/ppermute | solution.py:300
  36.6 4.0 all-to-all-start.1
  44.0 14.6 %collective-permute-done.1.chunk_ref = bf16[20,128,128]{2,1,0:T(8,128)(2,1)} collective-permute-done((bf16[20,128,128]{2,1,0:T(8,128)(2,1)S(1)}, bf16[20,128,128]{2,1,0:T(8,128)(2,1)}, u32[]{:S(2)}, u32[]{:S(2)}) %collective-permute-start.1) | collective-permute-done | bytes 655392 | tf_op jit(solution)/shard_map/ppermute | solution.py:300
  62.2 3.8 all-to-all-start.2
  69.5 15.0 %collective-permute-done.2.chunk_ref = bf16[20,128,128]{2,1,0:T(8,128)(2,1)S(1)} collective-permute-done((bf16[20,128,128]{2,1,0:T(8,128)(2,1)}, bf16[20,128,128]{2,1,0:T(8,128)(2,1)S(1)}, u32[]{:S(2)}, u32[]{:S(2)}) %collective-permute-start.2) | collective-permute-done | bytes 655392 | tf_op jit(solution)/shard_map/ppermute | solution.py:300
  89.0 4.3 all-to-all-start.3
  96.1 14.4 %all-to-all-done.3.refs_3_ = bf16[40,128,128]{2,1,0:T(8,128)(2,1)} async-done(((bf16[40,128,128]{2,1,0:T(8,128)(2,1)}), bf16[40,128,128]{2,1,0:T(8,128)(2,1)}, u32[]{:S(2)}, u32[]{:S(2)}) %all-to-all-start.3) | async-done | bytes 1310752 | tf_op jit(solution)/shard_map/all_to_all | solution.py:290
  110.5 4.6 all-to-all-start.10
  115.1 22.9 %arcs.2 = (bf16[40,128,128]{2,1,0:T(8,128)(2,1)}, bf16[40,128,128]{2,1,0:T(8,128)(2,1)}, bf16[40,128,128]{2,1,0:T(8,128)(2,1)}, bf16[40,128,128]{2,1,0:T(8,128)(2,1)}) custom-call(s32[72,128]{1,0:T(8,128)} %tables.1.tab_ref, bf16[40,128,128]{2,1,0:T(8,128)(2,1)} %copy-done.3, bf16[40,128,128]{2,1,0:T(8,128)(2,1)} %copy-done.4, ...), custom_call_target="tpu_custom_call" | custom-call | tf_op jit(solution)/shard_map/arcs/pallas_call | solution.py:222
  138.0 21.9 %all_to_all.110.got_ref = bf16[40,128,128]{2,1,0:T(8,128)(2,1)} all-to-all(bf16[40,128,128]{2,1,0:T(8,128)(2,1)} %get-tuple-element.15), channel_id=1, replica_groups={{0,1,2,3,4,5,6,7},{8,9,10,11,12,13,14,15},{16,17,18,19,20,21,22,23},{24..., dimensions={0} | all-to-all | bytes 2621440 | tf_op jit(solution)/shard_map/all_to_all | solution.py:290
  159.9 20.6 %all_to_all.111.got_ref = bf16[40,128,128]{2,1,0:T(8,128)(2,1)} all-to-all(bf16[40,128,128]{2,1,0:T(8,128)(2,1)S(1)} %copy-done.10), channel_id=1, replica_groups={{0,1,2,3,4,5,6,7},{8,9,10,11,12,13,14,15},{16,17,18,19,20,21,22,23},{24..., dimensions={0} | all-to-all | bytes 2621440 | tf_op jit(solution)/shard_map/all_to_all | solution.py:290
  180.5 3.6 all-to-all-start.5
  189.7 14.9 %collective-permute-done.3.refs_0_ = bf16[20,128,128]{2,1,0:T(8,128)(2,1)S(1)} collective-permute-done((bf16[20,128,128]{2,1,0:T(8,128)(2,1)}, bf16[20,128,128]{2,1,0:T(8,128)(2,1)S(1)}, u32[]{:S(2)}, u32[]{:S(2)}) %collective-permute-start.3) | collective-permute-done | bytes 655392 | tf_op jit(solution)/shard_map/ppermute | solution.py:312
  212.8 4.3 all-to-all-start.4
  217.1 8.7 %collective-permute-done.4.refs_0_ = bf16[20,128,128]{2,1,0:T(8,128)(2,1)S(1)} collective-permute-done((bf16[20,128,128]{2,1,0:T(8,128)(2,1)}, bf16[20,128,128]{2,1,0:T(8,128)(2,1)S(1)}, u32[]{:S(2)}, u32[]{:S(2)}) %collective-permute-start.4) | collective-permute-done | bytes 655392 | tf_op jit(solution)/shard_map/ppermute | solution.py:312
  238.2 8.5 %collective-permute-done.5.refs_0_ = bf16[20,128,128]{2,1,0:T(8,128)(2,1)S(1)} collective-permute-done((bf16[20,128,128]{2,1,0:T(8,128)(2,1)}, bf16[20,128,128]{2,1,0:T(8,128)(2,1)S(1)}, u32[]{:S(2)}, u32[]{:S(2)}) %collective-permute-start.5) | collective-permute-done | bytes 655392 | tf_op jit(solution)/shard_map/ppermute | solution.py:312
  247.6 5.3 fold.11
  252.9 4.0 convolution_bitcast_fusion.5
  260.6 5.2 all-to-all-start.8
  265.9 11.7 %cholesky.70 = f32[128,128]{1,0:T(8,128)S(1)} custom-call(f32[128,128]{1,0:T(8,128)S(1)} %fusion.19), custom_call_target="Cholesky" | custom-call | tf_op jit(solution)/shard_map/jit(cholesky)/cholesky | solution.py:351
  278.4 6.0 all-to-all-start.9
  285.8 9.8 %custom-call.10 = f32[1,128,128]{1,2,0:T(8,128)S(1)} custom-call(f32[1,128,128]{2,1,0:T(8,128)S(1)} %fusion.8), custom_call_target="InvertDiagBlocksLowerTriangular" | custom-call | tf_op jit(solution)/shard_map/jit(_cho_solve)/triangular_solve | solution.py:351
  295.7 11.7 %cholesky.59 = f32[128,128]{1,0:T(8,128)S(1)} custom-call(f32[128,128]{1,0:T(8,128)S(1)} %fusion.11), custom_call_target="Cholesky" | custom-call | tf_op jit(solution)/shard_map/jit(cholesky)/cholesky | solution.py:342
  308.8 9.8 %custom-call.9 = f32[1,128,128]{1,2,0:T(8,128)S(1)} custom-call(f32[1,128,128]{2,1,0:T(8,128)S(1)} %fusion.7), custom_call_target="InvertDiagBlocksLowerTriangular" | custom-call | tf_op jit(solution)/shard_map/jit(_cho_solve)/triangular_solve | solution.py:343
  326.8 4.4 all-to-all-start.12
  334.0 14.5 %collective-permute-done.6.chunk_ref = bf16[20,128,128]{2,1,0:T(8,128)(2,1)} collective-permute-done((bf16[20,128,128]{2,1,0:T(8,128)(2,1)S(1)}, bf16[20,128,128]{2,1,0:T(8,128)(2,1)}, u32[]{:S(2)}, u32[]{:S(2)}) %collective-permute-start.6) | collective-permute-done | bytes 655392 | tf_op jit(solution)/shard_map/ppermute | solution.py:300
  351.0 4.3 all-to-all-start.13
  358.8 14.8 %collective-permute-done.7.chunk_ref = bf16[20,128,128]{2,1,0:T(8,128)(2,1)S(1)} collective-permute-done((bf16[20,128,128]{2,1,0:T(8,128)(2,1)}, bf16[20,128,128]{2,1,0:T(8,128)(2,1)S(1)}, u32[]{:S(2)}, u32[]{:S(2)}) %collective-permute-start.7) | collective-permute-done | bytes 655392 | tf_op jit(solution)/shard_map/ppermute | solution.py:300
  376.9 4.4 all-to-all-start.14
  384.7 14.5 %collective-permute-done.8.chunk_ref = bf16[20,128,128]{2,1,0:T(8,128)(2,1)} collective-permute-done((bf16[20,128,128]{2,1,0:T(8,128)(2,1)S(1)}, bf16[20,128,128]{2,1,0:T(8,128)(2,1)}, u32[]{:S(2)}, u32[]{:S(2)}) %collective-permute-start.8) | collective-permute-done | bytes 655392 | tf_op jit(solution)/shard_map/ppermute | solution.py:300
  401.7 21.7 %all_to_all.112.refs_3_ = bf16[40,128,128]{2,1,0:T(8,128)(2,1)} all-to-all(bf16[40,128,128]{2,1,0:T(8,128)(2,1)} %pick.15), channel_id=1, replica_groups={{0,1,2,3,4,5,6,7},{8,9,10,11,12,13,14,15},{16,17,18,19,20,21,22,23},{24..., dimensions={0} | all-to-all | bytes 2621440 | tf_op jit(solution)/shard_map/all_to_all | solution.py:290
  423.4 22.9 %arcs.3 = (bf16[40,128,128]{2,1,0:T(8,128)(2,1)}, bf16[40,128,128]{2,1,0:T(8,128)(2,1)}, bf16[40,128,128]{2,1,0:T(8,128)(2,1)}, bf16[40,128,128]{2,1,0:T(8,128)(2,1)}) custom-call(s32[72,128]{1,0:T(8,128)} %tables.1.tab_ref, bf16[40,128,128]{2,1,0:T(8,128)(2,1)} %all-to-all-done.12.refs_0_, bf16[40,128,128]{2,1,0:T(8,128)(2,1)} %all-to-all-done.13.refs_1_, ...), custom_call_target="tpu_custom_call" | custom-call | tf_op jit(solution)/shard_map/arcs/pallas_call | solution.py:222
  446.3 21.9 %all_to_all.113.got_ref = bf16[40,128,128]{2,1,0:T(8,128)(2,1)} all-to-all(bf16[40,128,128]{2,1,0:T(8,128)(2,1)} %get-tuple-element.19), channel_id=1, replica_groups={{0,1,2,3,4,5,6,7},{8,9,10,11,12,13,14,15},{16,17,18,19,20,21,22,23},{24..., dimensions={0} | all-to-all | bytes 2621440 | tf_op jit(solution)/shard_map/all_to_all | solution.py:290
  468.2 20.6 %all_to_all.114.got_ref = bf16[40,128,128]{2,1,0:T(8,128)(2,1)} all-to-all(bf16[40,128,128]{2,1,0:T(8,128)(2,1)S(1)} %copy-done.11), channel_id=1, replica_groups={{0,1,2,3,4,5,6,7},{8,9,10,11,12,13,14,15},{16,17,18,19,20,21,22,23},{24..., dimensions={0} | all-to-all | bytes 2621440 | tf_op jit(solution)/shard_map/all_to_all | solution.py:290
  488.8 4.3 all-to-all-start.17
  496.0 3.6 collective-permute-start.9
  499.6 14.8 %collective-permute-done.9.refs_0_ = bf16[20,128,128]{2,1,0:T(8,128)(2,1)S(1)} collective-permute-done((bf16[20,128,128]{2,1,0:T(8,128)(2,1)}, bf16[20,128,128]{2,1,0:T(8,128)(2,1)S(1)}, u32[]{:S(2)}, u32[]{:S(2)}) %collective-permute-start.9) | collective-permute-done | bytes 655392 | tf_op jit(solution)/shard_map/ppermute | solution.py:312
  521.6 4.3 all-to-all-start.16
  525.9 9.7 %collective-permute-done.10.refs_0_ = bf16[20,128,128]{2,1,0:T(8,128)(2,1)S(1)} collective-permute-done((bf16[20,128,128]{2,1,0:T(8,128)(2,1)}, bf16[20,128,128]{2,1,0:T(8,128)(2,1)S(1)}, u32[]{:S(2)}, u32[]{:S(2)}) %collective-permute-start.10) | collective-permute-done | bytes 655392 | tf_op jit(solution)/shard_map/ppermute | solution.py:312
  543.2 12.8 %collective-permute-done.11.refs_0_ = bf16[20,128,128]{2,1,0:T(8,128)(2,1)S(1)} collective-permute-done((bf16[20,128,128]{2,1,0:T(8,128)(2,1)}, bf16[20,128,128]{2,1,0:T(8,128)(2,1)S(1)}, u32[]{:S(2)}, u32[]{:S(2)}) %collective-permute-start.11) | collective-permute-done | bytes 655392 | tf_op jit(solution)/shard_map/ppermute | solution.py:312
  556.9 5.3 fold.15
  562.2 3.9 fusion.1
  566.1 12.4 %all_to_all.115 = f32[32,4,128]{2,1,0:T(4,128)S(1)} all-to-all(f32[32,4,128]{2,1,0:T(4,128)S(1)} %bitcast.102), channel_id=1, replica_groups=mesh['arc'=8,'vec'=4] {'arc','vec'}, dimensions={0} | all-to-all | bytes 131072 | tf_op jit(solution)/shard_map/all_to_all | solution.py:29
  584.4 5.0 all-to-all-done.21
  589.5 11.7 %cholesky.81 = f32[128,128]{1,0:T(8,128)S(1)} custom-call(f32[128,128]{1,0:T(8,128)S(1)} %fusion.15), custom_call_target="Cholesky" | custom-call | tf_op jit(solution)/shard_map/jit(cholesky)/cholesky | solution.py:342
  602.6 9.8 %custom-call.11 = f32[1,128,128]{1,2,0:T(8,128)S(1)} custom-call(f32[1,128,128]{2,1,0:T(8,128)S(1)} %fusion.9), custom_call_target="InvertDiagBlocksLowerTriangular" | custom-call | tf_op jit(solution)/shard_map/jit(_cho_solve)/triangular_solve | solution.py:343
  612.9 4.1 convolution_subtract_fusion
  (135 shorter events, 126.0 us)
Async XLA Ops:
  10.7 5.3 copy-start.9
  10.7 25.9 %all-to-all-start = ((bf16[40,128,128]{2,1,0:T(8,128)(2,1)}), bf16[40,128,128]{2,1,0:T(8,128)(2,1)S(1)}, u32[]{:S(2)}, u32[]{:S(2)}) async-start(bf16[40,128,128]{2,1,0:T(8,128)(2,1)} %pick.8), calls=%async_computation | async-start | bytes 2621440 | tf_op jit(solution)/shard_map/all_to_all | solution.py:290
  16.0 17.2 %collective-permute-start = (bf16[20,128,128]{2,1,0:T(8,128)(2,1)S(1)}, bf16[20,128,128]{2,1,0:T(8,128)(2,1)S(1)}, u32[]{:S(2)}, u32[]{:S(2)}) collective-permute-start(bf16[20,128,128]{2,1,0:T(8,128)(2,1)S(1)} %copy-done.9), channel_id=1, source_target_pairs={{0,16},{1,17},{2,18},{3,19},{4,20},{5,21},{6,22},{7,23},{16,24},{1... | collective-permute-start | bytes 1966088 | tf_op jit(solution)/shard_map/ppermute | solution.py:300
  36.6 4.0 copy-start.13
  36.6 24.5 %copy-start.3 = (bf16[40,128,128]{2,1,0:T(8,128)(2,1)}, bf16[40,128,128]{2,1,0:T(8,128)(2,1)S(1)}, u32[]{:S(2)}) copy-start(bf16[40,128,128]{2,1,0:T(8,128)(2,1)S(1)} %all-to-all-done.refs_0_) | copy-start | bytes 3932164
  36.6 24.5 %all-to-all-start.1 = ((bf16[40,128,128]{2,1,0:T(8,128)(2,1)}), bf16[40,128,128]{2,1,0:T(8,128)(2,1)S(1)}, u32[]{:S(2)}, u32[]{:S(2)}) async-start(bf16[40,128,128]{2,1,0:T(8,128)(2,1)} %pick.9), calls=%async_computation.1 | async-start | bytes 2621440 | tf_op jit(solution)/shard_map/all_to_all | solution.py:290
  40.6 18.0 %collective-permute-start.1 = (bf16[20,128,128]{2,1,0:T(8,128)(2,1)S(1)}, bf16[20,128,128]{2,1,0:T(8,128)(2,1)}, u32[]{:S(2)}, u32[]{:S(2)}) collective-permute-start(bf16[20,128,128]{2,1,0:T(8,128)(2,1)S(1)} %copy-done.13), channel_id=1, source_target_pairs={{0,16},{1,17},{2,18},{3,19},{4,20},{5,21},{6,22},{7,23},{16,24},{1... | collective-permute-start | bytes 1966088 | tf_op jit(solution)/shard_map/ppermute | solution.py:300
  61.2 1.1 copy-start.4
  62.2 25.7 %all-to-all-start.2 = ((bf16[40,128,128]{2,1,0:T(8,128)(2,1)}), bf16[40,128,128]{2,1,0:T(8,128)(2,1)S(1)}, u32[]{:S(2)}, u32[]{:S(2)}) async-start(bf16[40,128,128]{2,1,0:T(8,128)(2,1)} %pick.10), calls=%async_computation.2 | async-start | bytes 2621440 | tf_op jit(solution)/shard_map/all_to_all | solution.py:290
  66.0 18.5 %collective-permute-start.2 = (bf16[20,128,128]{2,1,0:T(8,128)(2,1)}, bf16[20,128,128]{2,1,0:T(8,128)(2,1)S(1)}, u32[]{:S(2)}, u32[]{:S(2)}) collective-permute-start(bf16[20,128,128]{2,1,0:T(8,128)(2,1)} %collective-permute-done.1.chunk_ref), channel_id=1, source_target_pairs={{0,16},{1,17},{2,18},{3,19},{4,20},{5,21},{6,22},{7,23},{16,24},{1... | collective-permute-start | bytes 1966088 | tf_op jit(solution)/shard_map/ppermute | solution.py:300
  87.9 5.4 copy-start
  87.9 1.1 copy-start.5
  89.0 21.6 %all-to-all-start.3 = ((bf16[40,128,128]{2,1,0:T(8,128)(2,1)}), bf16[40,128,128]{2,1,0:T(8,128)(2,1)}, u32[]{:S(2)}, u32[]{:S(2)}) async-start(bf16[40,128,128]{2,1,0:T(8,128)(2,1)} %pick.11), calls=%async_computation.3 | async-start | bytes 2621440 | tf_op jit(solution)/shard_map/all_to_all | solution.py:290
  110.5 27.5 %all-to-all-start.10 = ((f32[32,4,128]{2,1,0:T(4,128)}), f32[32,4,128]{2,1,0:T(4,128)S(1)}, u32[]{:S(2)}, u32[]{:S(2)}) async-start(f32[32,4,128]{2,1,0:T(4,128)} %bitcast.9), calls=%async_computation.10 | async-start | bytes 131072 | tf_op jit(solution)/shard_map/all_to_all | solution.py:29
  138.0 21.9 %copy-start.10 = (bf16[40,128,128]{2,1,0:T(8,128)(2,1)S(1)}, bf16[40,128,128]{2,1,0:T(8,128)(2,1)}, u32[]{:S(2)}) copy-start(bf16[40,128,128]{2,1,0:T(8,128)(2,1)} %get-tuple-element.14) | copy-start | bytes 3932164
  180.5 31.3 %all-to-all-start.5 = ((bf16[40,128,128]{2,1,0:T(8,128)(2,1)}), bf16[40,128,128]{2,1,0:T(8,128)(2,1)S(1)}, u32[]{:S(2)}, u32[]{:S(2)}) async-start(bf16[40,128,128]{2,1,0:T(8,128)(2,1)} %get-tuple-element.13), calls=%async_computation.5 | async-start | bytes 2621440 | tf_op jit(solution)/shard_map/all_to_all | solution.py:290
  186.9 17.6 %collective-permute-start.3 = (bf16[20,128,128]{2,1,0:T(8,128)(2,1)}, bf16[20,128,128]{2,1,0:T(8,128)(2,1)S(1)}, u32[]{:S(2)}, u32[]{:S(2)}) collective-permute-start(bf16[20,128,128]{2,1,0:T(8,128)(2,1)} %fold.8), channel_id=1, source_target_pairs={{0,16},{1,17},{2,18},{3,19},{4,20},{5,21},{6,22},{7,23},{16,24},{1... | collective-permute-start | bytes 1966088 | tf_op jit(solution)/shard_map/ppermute | solution.py:312
  204.6 0.8 copy-start.21
  208.5 17.2 %collective-permute-start.4 = (bf16[20,128,128]{2,1,0:T(8,128)(2,1)}, bf16[20,128,128]{2,1,0:T(8,128)(2,1)S(1)}, u32[]{:S(2)}, u32[]{:S(2)}) collective-permute-start(bf16[20,128,128]{2,1,0:T(8,128)(2,1)} %fold.9), channel_id=1, source_target_pairs={{0,16},{1,17},{2,18},{3,19},{4,20},{5,21},{6,22},{7,23},{16,24},{1... | collective-permute-start | bytes 1966088 | tf_op jit(solution)/shard_map/ppermute | solution.py:312
  211.8 1.1 copy-start.6
  212.8 21.6 %all-to-all-start.4 = ((bf16[40,128,128]{2,1,0:T(8,128)(2,1)}), bf16[40,128,128]{2,1,0:T(8,128)(2,1)}, u32[]{:S(2)}, u32[]{:S(2)}) async-start(bf16[40,128,128]{2,1,0:T(8,128)(2,1)} %get-tuple-element.12), calls=%async_computation.4 | async-start | bytes 2621440 | tf_op jit(solution)/shard_map/all_to_all | solution.py:290
  225.8 0.8 copy-start.18
  229.7 17.1 %collective-permute-start.5 = (bf16[20,128,128]{2,1,0:T(8,128)(2,1)}, bf16[20,128,128]{2,1,0:T(8,128)(2,1)S(1)}, u32[]{:S(2)}, u32[]{:S(2)}) collective-permute-start(bf16[20,128,128]{2,1,0:T(8,128)(2,1)} %fold.10), channel_id=1, source_target_pairs={{0,16},{1,17},{2,18},{3,19},{4,20},{5,21},{6,22},{7,23},{16,24},{1... | collective-permute-start | bytes 1966088 | tf_op jit(solution)/shard_map/ppermute | solution.py:312
  235.0 25.6 %all-to-all-start.11 = ((f32[32,4,128]{2,1,0:T(4,128)}), f32[32,4,128]{2,1,0:T(4,128)S(1)}, u32[]{:S(2)}, u32[]{:S(2)}) async-start(f32[32,4,128]{2,1,0:T(4,128)} %broadcast_in_dim.7), calls=%async_computation.11 | async-start | bytes 131072 | tf_op jit(solution)/shard_map/all_to_all | solution.py:29
  238.2 14.7 %copy-start.23 = (f32[20,128]{1,0:T(8,128)S(1)}, f32[20,128]{1,0:T(8,128)}, u32[]{:S(2)}) copy-start(f32[20,128]{1,0:T(8,128)} %param.10) | copy-start | bytes 30724
  246.8 0.8 copy-start.17
  252.9 4.0 copy-start.1
  260.6 17.0 %all-to-all-start.8 = ((f32[32,12,128]{2,1,0:T(8,128)}), f32[32,12,128]{2,1,0:T(8,128)S(1)}, u32[]{:S(2)}, u32[]{:S(2)}) async-start(f32[32,12,128]{2,1,0:T(8,128)} %reshape.34), calls=%async_computation.8 | async-start | bytes 524288 | tf_op jit(solution)/shard_map/all_to_all | solution.py:29
  278.4 17.2 %all-to-all-start.9 = ((f32[32,12,128]{2,1,0:T(8,128)}), f32[32,12,128]{2,1,0:T(8,128)S(1)}, u32[]{:S(2)}, u32[]{:S(2)}) async-start(f32[32,12,128]{2,1,0:T(8,128)} %broadcast_in_dim.6), calls=%async_computation.9 | async-start | bytes 524288 | tf_op jit(solution)/shard_map/all_to_all | solution.py:29
  320.9 3.4 copy-start.2
  326.8 4.4 copy-start.8
  326.8 24.1 %all-to-all-start.12 = ((bf16[40,128,128]{2,1,0:T(8,128)(2,1)}), bf16[40,128,128]{2,1,0:T(8,128)(2,1)}, u32[]{:S(2)}, u32[]{:S(2)}) async-start(bf16[40,128,128]{2,1,0:T(8,128)(2,1)} %pick.12), calls=%async_computation.12 | async-start | bytes 2621440 | tf_op jit(solution)/shard_map/all_to_all | solution.py:290
  331.2 17.2 %collective-permute-start.6 = (bf16[20,128,128]{2,1,0:T(8,128)(2,1)S(1)}, bf16[20,128,128]{2,1,0:T(8,128)(2,1)}, u32[]{:S(2)}, u32[]{:S(2)}) collective-permute-start(bf16[20,128,128]{2,1,0:T(8,128)(2,1)S(1)} %copy-done.8), channel_id=1, source_target_pairs={{0,16},{1,17},{2,18},{3,19},{4,20},{5,21},{6,22},{7,23},{16,24},{1... | collective-permute-start | bytes 1966088 | tf_op jit(solution)/shard_map/ppermute | solution.py:300
  351.0 26.0 %all-to-all-start.13 = ((bf16[40,128,128]{2,1,0:T(8,128)(2,1)}), bf16[40,128,128]{2,1,0:T(8,128)(2,1)}, u32[]{:S(2)}, u32[]{:S(2)}) async-start(bf16[40,128,128]{2,1,0:T(8,128)(2,1)} %pick.13), calls=%async_computation.13 | async-start | bytes 2621440 | tf_op jit(solution)/shard_map/all_to_all | solution.py:290
  355.2 18.3 %collective-permute-start.7 = (bf16[20,128,128]{2,1,0:T(8,128)(2,1)}, bf16[20,128,128]{2,1,0:T(8,128)(2,1)S(1)}, u32[]{:S(2)}, u32[]{:S(2)}) collective-permute-start(bf16[20,128,128]{2,1,0:T(8,128)(2,1)} %collective-permute-done.6.chunk_ref), channel_id=1, source_target_pairs={{0,16},{1,17},{2,18},{3,19},{4,20},{5,21},{6,22},{7,23},{16,24},{1... | collective-permute-start | bytes 1966088 | tf_op jit(solution)/shard_map/ppermute | solution.py:300
  376.9 4.4 copy-start.15
  376.9 24.7 %all-to-all-start.14 = ((bf16[40,128,128]{2,1,0:T(8,128)(2,1)}), bf16[40,128,128]{2,1,0:T(8,128)(2,1)}, u32[]{:S(2)}, u32[]{:S(2)}) async-start(bf16[40,128,128]{2,1,0:T(8,128)(2,1)} %pick.14), calls=%async_computation.14 | async-start | bytes 2621440 | tf_op jit(solution)/shard_map/all_to_all | solution.py:290
  381.3 17.8 %collective-permute-start.8 = (bf16[20,128,128]{2,1,0:T(8,128)(2,1)S(1)}, bf16[20,128,128]{2,1,0:T(8,128)(2,1)}, u32[]{:S(2)}, u32[]{:S(2)}) collective-permute-start(bf16[20,128,128]{2,1,0:T(8,128)(2,1)S(1)} %copy-done.15), channel_id=1, source_target_pairs={{0,16},{1,17},{2,18},{3,19},{4,20},{5,21},{6,22},{7,23},{16,24},{1... | collective-permute-start | bytes 1966088 | tf_op jit(solution)/shard_map/ppermute | solution.py:300
  446.3 21.9 %copy-start.11 = (bf16[40,128,128]{2,1,0:T(8,128)(2,1)S(1)}, bf16[40,128,128]{2,1,0:T(8,128)(2,1)}, u32[]{:S(2)}) copy-start(bf16[40,128,128]{2,1,0:T(8,128)(2,1)} %get-tuple-element.18) | copy-start | bytes 3932164
  488.8 32.8 %all-to-all-start.17 = ((bf16[40,128,128]{2,1,0:T(8,128)(2,1)}), bf16[40,128,128]{2,1,0:T(8,128)(2,1)}, u32[]{:S(2)}, u32[]{:S(2)}) async-start(bf16[40,128,128]{2,1,0:T(8,128)(2,1)} %get-tuple-element.17), calls=%async_computation.17 | async-start | bytes 2621440 | tf_op jit(solution)/shard_map/all_to_all | solution.py:290
  496.0 18.4 %collective-permute-start.9 = (bf16[20,128,128]{2,1,0:T(8,128)(2,1)}, bf16[20,128,128]{2,1,0:T(8,128)(2,1)S(1)}, u32[]{:S(2)}, u32[]{:S(2)}) collective-permute-start(bf16[20,128,128]{2,1,0:T(8,128)(2,1)} %fold.12), channel_id=1, source_target_pairs={{0,16},{1,17},{2,18},{3,19},{4,20},{5,21},{6,22},{7,23},{16,24},{1... | collective-permute-start | bytes 1966088 | tf_op jit(solution)/shard_map/ppermute | solution.py:312
  514.4 0.8 copy-start.22
  518.4 17.2 %collective-permute-start.10 = (bf16[20,128,128]{2,1,0:T(8,128)(2,1)}, bf16[20,128,128]{2,1,0:T(8,128)(2,1)S(1)}, u32[]{:S(2)}, u32[]{:S(2)}) collective-permute-start(bf16[20,128,128]{2,1,0:T(8,128)(2,1)} %fold.13), channel_id=1, source_target_pairs={{0,16},{1,17},{2,18},{3,19},{4,20},{5,21},{6,22},{7,23},{16,24},{1... | collective-permute-start | bytes 1966088 | tf_op jit(solution)/shard_map/ppermute | solution.py:312
  521.6 21.6 %all-to-all-start.16 = ((bf16[40,128,128]{2,1,0:T(8,128)(2,1)}), bf16[40,128,128]{2,1,0:T(8,128)(2,1)}, u32[]{:S(2)}, u32[]{:S(2)}) async-start(bf16[40,128,128]{2,1,0:T(8,128)(2,1)} %get-tuple-element.16), calls=%async_computation.16 | async-start | bytes 2621440 | tf_op jit(solution)/shard_map/all_to_all | solution.py:290
  535.6 0.8 copy-start.19
  539.5 16.5 %collective-permute-start.11 = (bf16[20,128,128]{2,1,0:T(8,128)(2,1)}, bf16[20,128,128]{2,1,0:T(8,128)(2,1)S(1)}, u32[]{:S(2)}, u32[]{:S(2)}) collective-permute-start(bf16[20,128,128]{2,1,0:T(8,128)(2,1)} %fold.14), channel_id=1, source_target_pairs={{0,16},{1,17},{2,18},{3,19},{4,20},{5,21},{6,22},{7,23},{16,24},{1... | collective-permute-start | bytes 1966088 | tf_op jit(solution)/shard_map/ppermute | solution.py:312
  579.2 10.2 %all-to-all-start.21 = ((f32[32,4,128]{2,1,0:T(4,128)}), f32[32,4,128]{2,1,0:T(4,128)S(1)}, u32[]{:S(2)}, u32[]{:S(2)}) async-start(f32[32,4,128]{2,1,0:T(4,128)} %broadcast_in_dim.8), calls=%async_computation.21 | async-start | bytes 131072 | tf_op jit(solution)/shard_map/all_to_all | solution.py:29
  612.9 4.1 copy-start.7
  (4 other events, 3.3 us)
